TPU v7x, 256 devices: a whole 4x4x8 slice. The times are simulated.
256 devices in a mesh: grp: 8 (over x_lo, y), slab: 32 (over x_hi, z, core).
Axes of the slice: x: 4 (x_hi: 2, x_lo: 2; x = x_hi * 2 + x_lo), y: 4, z: 8, core: 2. Of those that a mesh axis runs over, the one named last changes fastest.
Arguments:
- template: float32 [256, 64, 256], P('slab'), may hold values from -6 to 6
- images: bfloat16 [32, 256, 64, 256], P('grp', 'slab'), may hold values from -6 to 6
- velocity: float32 [32, 3, 256, 64, 256], P('grp', None, 'slab'), may hold values from -3 to 3
- labels: int32 [256, 64, 256], P('slab'), may hold values from 0 to 3
- stiffness: float32 [4], replicated, may hold values from 0.5 to 2
- cohort: int32 [32], P('grp'), may hold values from 0 to 7
- site_gain: float32 [8], replicated, may hold values from 0.5 to 2
Outputs:
- new_template: float32 [256, 64, 256], P('slab')
- new_velocity: float32 [32, 3, 256, 64, 256], P('grp', None, 'slab')
All inputs are finite; a program needn't handle non-finite values.
Results may differ from a plain program's by a relative error of at most 0.0003.
Values sent between devices are 32-bit elements; how exact they have to be, the bound alone decides.
No kernel may reach another device: no remote copies, remote signals or barrier semaphores. Data moves between devices by JAX's collectives and lax.ppermute only.
A program may use at most 64 MiB of HBM per device.

v0:
```python
import jax
import jax.numpy as jnp
from jax import lax
from jax.sharding import PartitionSpec as P

velocity_step = 0.05
template_step = 0.5


def extended(block, sides, width):
    for axis, dim in sides:
        count = lax.axis_size(axis)
        forward = [(i, i + 1) for i in range(count - 1)]
        backward = [(target, source) for source, target in forward]
        low = lax.ppermute(
            lax.slice_in_dim(block, block.shape[dim] - width, None, axis=dim), axis, forward
        )
        high = lax.ppermute(lax.slice_in_dim(block, 0, width, axis=dim), axis, backward)
        block = jnp.concatenate([low, block, high], axis=dim)
    return block


def slopes_of(padded):
    along_z = 0.5 * (padded[..., 2:, 1:-1, 1:-1] - padded[..., :-2, 1:-1, 1:-1])
    along_y = 0.5 * (padded[..., 1:-1, 2:, 1:-1] - padded[..., 1:-1, :-2, 1:-1])
    along_x = 0.5 * (padded[..., 1:-1, 1:-1, 2:] - padded[..., 1:-1, 1:-1, :-2])
    return jnp.stack([along_z, along_y, along_x], axis=-4)


def around_of(padded):
    beside_all = padded[..., 2:, 1:-1, 1:-1] + padded[..., :-2, 1:-1, 1:-1]
    beside_all = beside_all + padded[..., 1:-1, 2:, 1:-1] + padded[..., 1:-1, :-2, 1:-1]
    return beside_all + padded[..., 1:-1, 1:-1, 2:] + padded[..., 1:-1, 1:-1, :-2]


def pad_plane(field):
    return jnp.pad(field, [(0, 0)] * (field.ndim - 2) + [(1, 1), (1, 1)])


def local(template, images, velocity, labels, stiffness, cohort, site_gain):
    template_wide = extended(template, (("slab", 0),), 1)
    velocity_wide = extended(velocity, (("slab", 2),), 1)
    slopes = slopes_of(pad_plane(template_wide))
    levels = jnp.arange(stiffness.shape[0], dtype=jnp.int32)
    stiff_map = jnp.sum(
        jnp.where(labels[None] == levels[:, None, None, None], stiffness[:, None, None, None], 0.0),
        axis=0,
    )
    groups = jnp.arange(site_gain.shape[0], dtype=jnp.int32)
    subject_gain = jnp.sum(
        jnp.where(cohort[:, None] == groups[None, :], site_gain[None, :], 0.0), axis=1
    )
    warped = template[None] + jnp.sum(slopes[None] * velocity, axis=1)
    residual = warped - subject_gain[:, None, None, None] * images.astype(jnp.float32)
    elastic = stiff_map * (6.0 * velocity - around_of(pad_plane(velocity_wide)))
    new_velocity = velocity - velocity_step * (residual[:, None] * slopes[None] + elastic)
    group_partial = jnp.sum(residual, axis=0)
    subjects = images.shape[0] * lax.axis_size("grp")
    share = lax.psum_scatter(group_partial, "grp", scatter_dimension=1, tiled=True)
    share_rows = share.shape[1]
    own_rows = lax.dynamic_slice_in_dim(template, lax.axis_index("grp") * share_rows, share_rows, 1)
    new_template = lax.all_gather(
        own_rows - template_step * share / subjects, "grp", axis=1, tiled=True
    )
    return (new_template, new_velocity)


def solution(mesh):
    placed = (
        P("slab", None, None),
        P("grp", "slab", None, None),
        P("grp", None, "slab", None, None),
        P("slab", None, None),
        P(),
        P("grp"),
        P(),
    )
    return jax.shard_map(
        local,
        mesh=mesh,
        in_specs=placed,
        out_specs=(P("slab", None, None), P("grp", None, "slab", None, None)),
        check_vma=False,
    )
```

profile of v0, /device:TPU:4, one launch (start us, length us, event | category | flops | bytes accessed | tf_op | source)
XLA Modules:
  0.0 113.6 jit_solution(6247605921446230556)
XLA Ops:
  7.2 0.0 copy-start.2
  7.2 0.0 reduce-scatter.2.cloned.1.call-start
  7.2 0.9 fusion.21
  8.2 1.9 %collective-permute-start.1 = (f32[1,64,256]{2,1,0:T(8,128)S(1)}, f32[1,64,256]{2,1,0:T(8,128)S(1)}, u32[]{:S(2)}, u32[]{:S(2)}) collective-permute-start(f32[1,64,256]{2,1,0:T(8,128)S(1)} %get-tuple-element.8), channel_id=1, source_target_pairs={{0,1},{1,2},{2,3},{3,4},{4,5},{5,6},{6,7},{7,8},{8,9},{9,10},{10,1... | collective-permute-start | bytes 196616 | tf_op jit(solution)/shard_map/ppermute | solution.py:15
  10.1 7.3 %collective-permute-start = (f32[1,64,256]{2,1,0:T(8,128)S(1)}, f32[1,64,256]{2,1,0:T(8,128)S(1)}, u32[]{:S(2)}, u32[]{:S(2)}) collective-permute-start(f32[1,64,256]{2,1,0:T(8,128)S(1)} %get-tuple-element.9), channel_id=1, source_target_pairs={{1,0},{2,1},{3,2},{4,3},{5,4},{6,5},{7,6},{8,7},{9,8},{10,9},{11,1... | collective-permute-start | bytes 196616 | tf_op jit(solution)/shard_map/ppermute | solution.py:18
  17.3 2.7 %fusion.20 = (f32[4,3,1,64,256]{4,3,2,1,0:T(8,128)}, f32[4,3,1,64,256]{4,3,2,1,0:T(8,128)}) fusion(f32[4,3,8,64,256]{4,3,2,1,0:T(8,128)} %param.9), kind=kLoop, calls=%fused_computation.50 | loop fusion | bytes 3145728 | tf_op jit(solution)/shard_map/slice | solution.py:16
  20.0 1.9 %collective-permute-start.3 = (f32[4,3,1,64,256]{4,3,2,1,0:T(8,128)}, f32[4,3,1,64,256]{4,3,2,1,0:T(8,128)S(1)}, u32[]{:S(2)}, u32[]{:S(2)}) collective-permute-start(f32[4,3,1,64,256]{4,3,2,1,0:T(8,128)} %get-tuple-element.4), channel_id=1, source_target_pairs={{0,1},{1,2},{2,3},{3,4},{4,5},{5,6},{6,7},{7,8},{8,9},{9,10},{10,1... | collective-permute-start | bytes 2359304 | tf_op jit(solution)/shard_map/ppermute | solution.py:15
  22.0 7.3 %collective-permute-start.2 = (f32[4,3,1,64,256]{4,3,2,1,0:T(8,128)}, f32[4,3,1,64,256]{4,3,2,1,0:T(8,128)}, u32[]{:S(2)}, u32[]{:S(2)}) collective-permute-start(f32[4,3,1,64,256]{4,3,2,1,0:T(8,128)} %get-tuple-element.5), channel_id=1, source_target_pairs={{1,0},{2,1},{3,2},{4,3},{5,4},{6,5},{7,6},{8,7},{9,8},{10,9},{11,1... | collective-permute-start | bytes 2359304 | tf_op jit(solution)/shard_map/ppermute | solution.py:18
  29.2 1.5 %select_reduce_fusion = f32[8,64,256]{2,1,0:T(8,128)S(1)} fusion(f32[4]{0:T(128)} %param.11, s32[8,64,256]{2,1,0:T(8,128)} %param.10), kind=kLoop, calls=%fused_computation.22 | loop fusion | flops 1441792 | bytes 1048592 | tf_op jit(solution)/shard_map/reduce_sum | solution.py:45
  30.8 1.2 %select_reduce_fusion.1 = f32[4]{0:T(128)S(1)} fusion(f32[8]{0:T(128)} %param.13, s32[4]{0:T(128)} %param.12), kind=kLoop, calls=%fused_computation.47 | loop fusion | flops 92 | bytes 64 | tf_op jit(solution)/shard_map/reduce_sum | solution.py:50
  32.0 1.4 %select_maximum_fusion.2 = f32[10,66,258]{2,1,0:T(8,128)S(1)} fusion(f32[1,64,256]{2,1,0:T(8,128)S(1)} %collective-permute-done, f32[8,64,256]{2,1,0:T(8,128)} %param.7, f32[1,64,256]{2,1,0:T(8,128)S(1)} %collective-permute-done.1), kind=kLoop, calls=%fused_computation.30 | loop fusion | flops 2554200 | bytes 1336480 | tf_op jit(solution)/shard_map/concatenate | solution.py:19
  33.4 0.5 fusion.15
  34.0 0.1 pad_maximum_fusion.2
  34.1 1.1 multiply_reduce_fusion
  35.2 0.0 copy-done.3
  35.2 2.6 %fusion.19 = (f32[8,64,256]{2,1,0:T(8,128)}, f32[4,8,64,256]{3,2,1,0:T(8,128)}) fusion(bf16[4,8,64,256]{3,2,1,0:T(8,128)(2,1)S(1)} %copy-done.3, f32[4]{0:T(128)S(1)} %select_reduce_fusion.1, f32[4,8,64,256]{3,2,1,0:T(8,128)S(1)} %multiply_reduce_fusion, f32[8,64,256]{2,1,0:T(8,128)S(1)} %copy-done.2), kind=kLoop, calls=%fused_computation.49 | loop fusion | flops 2490368 | bytes 6291472 | tf_op jit(solution)/shard_map/reduce_sum | solution.py:57
  37.9 0.0 reduce-scatter.2.cloned.1.call-update
  37.9 1.1 collective-permute-done.2
  39.0 7.6 %select_maximum_fusion = f32[4,3,10,66,258]{4,3,2,1,0:T(8,128)S(1)} fusion(f32[4,3,1,64,256]{4,3,2,1,0:T(8,128)} %collective-permute-done.2, f32[4,3,8,64,256]{4,3,2,1,0:T(8,128)} %param.9, f32[4,3,1,64,256]{4,3,2,1,0:T(8,128)S(1)} %collective-permute-done.3), kind=kLoop, calls=%fused_computation.4 | loop fusion | flops 30650400 | bytes 16037760 | tf_op jit(solution)/shard_map/concatenate | solution.py:19
  46.6 12.5 %fusion.7 = f32[4,3,8,64,256]{4,3,2,1,0:T(8,128)} fusion(f32[4,3,8,64,256]{4,3,2,1,0:T(8,128)} %param.9, f32[4,3,10,66,258]{4,3,2,1,0:T(8,128)S(1)} %select_maximum_fusion, f32[4,3,1,64,256]{4,3,2,1,0:T(8,128)S(1)} %collective-permute-done.3, f32[4,3,1,64,256]{4,3,2,1,0:T(8,128)} %collective-permute-done.2, f32[8,64,256]{2,1,0:T(8,128)S(1)} %select_reduce_fusion, ...), kind=kLoop, calls=%fused_computation.14 | loop fusion | flops 22020096 | bytes 43515904 | tf_op jit(solution)/shard_map/sub | solution.py:56
  59.1 17.0 %reduce-scatter.2.cloned.1.call-done = f32[8,8,256]{2,1,0:T(8,128)} async-done(((f32[8,64,256]{2,1,0:T(8,128)}), f32[8,8,256]{2,1,0:T(8,128)}) %reduce-scatter.2.cloned.1.call-update) | async-done | bytes 65552 | tf_op jit(solution)/shard_map/reduce_scatter | solution.py:59
  76.1 0.8 multiply_subtract_fusion.1
  77.0 29.0 %all_gather.3 = f32[8,64,256]{2,1,0:T(8,128)S(1)} all-gather(f32[8,8,256]{2,1,0:T(8,128)S(1)} %multiply_subtract_fusion.1), channel_id=1, replica_groups=mesh['grp'=8,'slab'=32] {'grp'}, dimensions={1}, use_global_device_ids=true | all-gather | bytes 589824 | tf_op jit(solution)/shard_map/all_gather | solution.py:62
  106.0 0.8 copy.10
  (10 shorter events, 0.1 us)
Async XLA Ops:
  7.2 26.8 %copy-start.2 = (f32[8,64,256]{2,1,0:T(8,128)S(1)}, f32[8,64,256]{2,1,0:T(8,128)}, u32[]{:S(2)}) copy-start(f32[8,64,256]{2,1,0:T(8,128)} %param.7) | copy-start | bytes 1572868
  7.2 68.9 %reduce-scatter.2.cloned.1.call-start = ((), (), s32[]{:S(2)}) async-start(), calls=%async_computation.1 | async-start | bytes 589824 | tf_op jit(solution)/shard_map/reduce_scatter | solution.py:59
  8.2 23.9 %collective-permute-start.1 = (f32[1,64,256]{2,1,0:T(8,128)S(1)}, f32[1,64,256]{2,1,0:T(8,128)S(1)}, u32[]{:S(2)}, u32[]{:S(2)}) collective-permute-start(f32[1,64,256]{2,1,0:T(8,128)S(1)} %get-tuple-element.8), channel_id=1, source_target_pairs={{0,1},{1,2},{2,3},{3,4},{4,5},{5,6},{6,7},{7,8},{8,9},{9,10},{10,1... | collective-permute-start | bytes 196616 | tf_op jit(solution)/shard_map/ppermute | solution.py:15
  10.1 21.9 %collective-permute-start = (f32[1,64,256]{2,1,0:T(8,128)S(1)}, f32[1,64,256]{2,1,0:T(8,128)S(1)}, u32[]{:S(2)}, u32[]{:S(2)}) collective-permute-start(f32[1,64,256]{2,1,0:T(8,128)S(1)} %get-tuple-element.9), channel_id=1, source_target_pairs={{1,0},{2,1},{3,2},{4,3},{5,4},{6,5},{7,6},{8,7},{9,8},{10,9},{11,1... | collective-permute-start | bytes 196616 | tf_op jit(solution)/shard_map/ppermute | solution.py:18
  20.0 17.9 %collective-permute-start.3 = (f32[4,3,1,64,256]{4,3,2,1,0:T(8,128)}, f32[4,3,1,64,256]{4,3,2,1,0:T(8,128)S(1)}, u32[]{:S(2)}, u32[]{:S(2)}) collective-permute-start(f32[4,3,1,64,256]{4,3,2,1,0:T(8,128)} %get-tuple-element.4), channel_id=1, source_target_pairs={{0,1},{1,2},{2,3},{3,4},{4,5},{5,6},{6,7},{7,8},{8,9},{9,10},{10,1... | collective-permute-start | bytes 2359304 | tf_op jit(solution)/shard_map/ppermute | solution.py:15
  22.0 17.1 %collective-permute-start.2 = (f32[4,3,1,64,256]{4,3,2,1,0:T(8,128)}, f32[4,3,1,64,256]{4,3,2,1,0:T(8,128)}, u32[]{:S(2)}, u32[]{:S(2)}) collective-permute-start(f32[4,3,1,64,256]{4,3,2,1,0:T(8,128)} %get-tuple-element.5), channel_id=1, source_target_pairs={{1,0},{2,1},{3,2},{4,3},{5,4},{6,5},{7,6},{8,7},{9,8},{10,9},{11,1... | collective-permute-start | bytes 2359304 | tf_op jit(solution)/shard_map/ppermute | solution.py:18
  29.2 4.9 %copy-start = (f32[4,3,8,64,256]{4,3,2,1,0:T(8,128)S(1)}, f32[4,3,8,64,256]{4,3,2,1,0:T(8,128)}, u32[]{:S(2)}) copy-start(f32[4,3,8,64,256]{4,3,2,1,0:T(8,128)} %param.9) | copy-start | bytes 18874372
  34.0 1.2 %copy-start.3 = (bf16[4,8,64,256]{3,2,1,0:T(8,128)(2,1)S(1)}, bf16[4,8,64,256]{3,2,1,0:T(8,128)(2,1)}, u32[]{:S(2)}) copy-start(bf16[4,8,64,256]{3,2,1,0:T(8,128)(2,1)} %param.8) | copy-start | bytes 3145732
  37.9 8.7 %copy-start.1 = (f32[4,8,64,256]{3,2,1,0:T(8,128)S(1)}, f32[4,8,64,256]{3,2,1,0:T(8,128)}, u32[]{:S(2)}) copy-start(f32[4,8,64,256]{3,2,1,0:T(8,128)} %get-tuple-element.3) | copy-start | bytes 6291460
Sparse Core Ops, SparseCore 0:
  38.0 38.0 reduce-scatter.1
where the time goes:
time: 114 us
  other arithmetic  29.5 us (26%)
  blocking collectives  29 us (25%)
  starting transfers between devices  18.4 us (16%)
  waiting for transfers between devices  18.1 us (16%)
  between operations  14.2 us (12%)
  local copies, waits for them, and re-layouts  4.45 us (4%)
    all_gather x1, blocking collectives, local(): lax.all_gather(own_rows - template_step * share / subjects, 'grp', axis=1...  29 us
    reduce_scatter x1, waiting for transfers between devices, local(): lax.psum_scatter(group_partial, 'grp', scatter_dimension=1, tiled=True)  17 us
    ppermute x2, starting transfers between devices, extended(): lax.ppermute(lax.slice_in_dim(block, 0, width, axis=dim), axis, backward)  14.5 us
    sub x1, other arithmetic, local(): velocity - velocity_step * (residual[:, None] * slopes[None] + elastic)  12.5 us
    concatenate x2, other arithmetic, extended(): block = jnp.concatenate([low, block, high], axis=dim)  8.97 us
    ppermute x2, starting transfers between devices, extended(): lax.ppermute(lax.slice_in_dim(block, block.shape[dim] - width, None, axis...  3.83 us
    slice x2, local copies, waits for them, and re-layouts, extended(): lax.slice_in_dim(block, block.shape[dim] - width, None, axis=dim)  3.62 us
    reduce_sum x1, other arithmetic, local(): group_partial = jnp.sum(residual, axis=0)  2.64 us
  transfers between devices with their start and end apart: 5, of which 2 were waited for; matrix products, arithmetic and copies ran while one was open for 28% of the time, Pallas kernels for 0%

commit v1 on v0

--- a/solution.py
+++ b/solution.py
@@ -59,8 +59,14 @@
     share = lax.psum_scatter(group_partial, "grp", scatter_dimension=1, tiled=True)
     share_rows = share.shape[1]
     own_rows = lax.dynamic_slice_in_dim(template, lax.axis_index("grp") * share_rows, share_rows, 1)
-    new_template = lax.all_gather(
-        own_rows - template_step * share / subjects, "grp", axis=1, tiled=True
+    new_template = jnp.concatenate(
+        lax.all_to_all(
+            jnp.stack([own_rows - template_step * share / subjects] * lax.axis_size("grp")),
+            "grp",
+            0,
+            0,
+        ),
+        axis=1,
     )
     return (new_template, new_velocity)
 

time: 114 us -> 116 us (1.018)
  blocking collectives: 29 us -> 0 us
  other arithmetic: 29.5 us -> 45.8 us
  waiting for transfers between devices: 18.1 us -> 27.5 us
  starting transfers between devices: 18.4 us -> 21.9 us
    all_gather x1 -> x0, blocking collectives: 29 us -> none  [local(): lax.all_gather(own_rows - template_step * share / subjects, 'grp', axis=1...]
    sub x1, other arithmetic: 12.5 us -> 25.7 us  [local(): velocity - velocity_step * (residual[:, None] * slopes[None] + elastic)]
    reduce_scatter x1, waiting for transfers between devices: 17 us -> 26.3 us  [local(): lax.psum_scatter(group_partial, 'grp', scatter_dimension=1, tiled=True)]
    all_to_all x0 -> x1, starting transfers between devices: none -> 3.49 us  [local(): lax.all_to_all(jnp.stack([own_rows - template_step * share / subjects] *...]
    concatenate x2, other arithmetic: 8.97 us -> 12.2 us  [extended(): block = jnp.concatenate([low, block, high], axis=dim)]
  transfers between devices with their start and end apart: 5 -> 6, of which waited for: 2 -> 2; matrix products, arithmetic and copies ran while one was open for 28% -> 42% of each run, Pallas kernels for 0% -> 0%
where the time goes in v1:
time: 116 us; the launch traced here: 115 us
  other arithmetic  45.8 us (39%)
  waiting for transfers between devices  27.5 us (24%)
  starting transfers between devices  21.9 us (19%)
  between operations  14.2 us (12%)
  local copies, waits for them, and re-layouts  5.32 us (5%)
    reduce_scatter x1, waiting for transfers between devices, local(): lax.psum_scatter(group_partial, 'grp', scatter_dimension=1, tiled=True)  26.3 us
    sub x1, other arithmetic, local(): velocity - velocity_step * (residual[:, None] * slopes[None] + elastic)  25.7 us
    ppermute x2, starting transfers between devices, extended(): lax.ppermute(lax.slice_in_dim(block, 0, width, axis=dim), axis, backward)  14.5 us
    concatenate x2, other arithmetic, extended(): block = jnp.concatenate([low, block, high], axis=dim)  12.2 us
    ppermute x2, starting transfers between devices, extended(): lax.ppermute(lax.slice_in_dim(block, block.shape[dim] - width, None, axis...  3.83 us
    slice x2, local copies, waits for them, and re-layouts, extended(): lax.slice_in_dim(block, block.shape[dim] - width, None, axis=dim)  3.6 us
    all_to_all x1, starting transfers between devices, local(): lax.all_to_all(jnp.stack([own_rows - template_step * share / subjects] *...  3.49 us
    reduce_sum x1, other arithmetic, local(): group_partial = jnp.sum(residual, axis=0)  2.62 us
  transfers between devices with their start and end apart: 6, of which 2 were waited for; matrix products, arithmetic and copies ran while one was open for 42% of the time, Pallas kernels for 0%

profile of v1, /device:TPU:4, one launch (start us, length us, event | category | flops | bytes accessed | tf_op | source)
XLA Modules:
  0.0 114.7 jit_solution(17198903695313846229)
XLA Ops:
  7.2 0.0 reduce-scatter.2.cloned.1.call-start
  7.2 0.9 fusion.21
  8.2 1.9 %collective-permute-start.1 = (f32[1,64,256]{2,1,0:T(8,128)S(1)}, f32[1,64,256]{2,1,0:T(8,128)S(1)}, u32[]{:S(2)}, u32[]{:S(2)}) collective-permute-start(f32[1,64,256]{2,1,0:T(8,128)S(1)} %get-tuple-element.8), channel_id=1, source_target_pairs={{0,1},{1,2},{2,3},{3,4},{4,5},{5,6},{6,7},{7,8},{8,9},{9,10},{10,1... | collective-permute-start | bytes 196616 | tf_op jit(solution)/shard_map/ppermute | solution.py:15
  10.1 7.3 %collective-permute-start = (f32[1,64,256]{2,1,0:T(8,128)S(1)}, f32[1,64,256]{2,1,0:T(8,128)S(1)}, u32[]{:S(2)}, u32[]{:S(2)}) collective-permute-start(f32[1,64,256]{2,1,0:T(8,128)S(1)} %get-tuple-element.9), channel_id=1, source_target_pairs={{1,0},{2,1},{3,2},{4,3},{5,4},{6,5},{7,6},{8,7},{9,8},{10,9},{11,1... | collective-permute-start | bytes 196616 | tf_op jit(solution)/shard_map/ppermute | solution.py:18
  17.3 2.7 %fusion.20 = (f32[4,3,1,64,256]{4,3,2,1,0:T(8,128)}, f32[4,3,1,64,256]{4,3,2,1,0:T(8,128)}) fusion(f32[4,3,8,64,256]{4,3,2,1,0:T(8,128)} %param.9), kind=kLoop, calls=%fused_computation.51 | loop fusion | bytes 3145728 | tf_op jit(solution)/shard_map/slice | solution.py:16
  20.0 1.9 %collective-permute-start.3 = (f32[4,3,1,64,256]{4,3,2,1,0:T(8,128)}, f32[4,3,1,64,256]{4,3,2,1,0:T(8,128)S(1)}, u32[]{:S(2)}, u32[]{:S(2)}) collective-permute-start(f32[4,3,1,64,256]{4,3,2,1,0:T(8,128)} %get-tuple-element.4), channel_id=1, source_target_pairs={{0,1},{1,2},{2,3},{3,4},{4,5},{5,6},{6,7},{7,8},{8,9},{9,10},{10,1... | collective-permute-start | bytes 2359304 | tf_op jit(solution)/shard_map/ppermute | solution.py:15
  21.9 7.3 %collective-permute-start.2 = (f32[4,3,1,64,256]{4,3,2,1,0:T(8,128)}, f32[4,3,1,64,256]{4,3,2,1,0:T(8,128)}, u32[]{:S(2)}, u32[]{:S(2)}) collective-permute-start(f32[4,3,1,64,256]{4,3,2,1,0:T(8,128)} %get-tuple-element.5), channel_id=1, source_target_pairs={{1,0},{2,1},{3,2},{4,3},{5,4},{6,5},{7,6},{8,7},{9,8},{10,9},{11,1... | collective-permute-start | bytes 2359304 | tf_op jit(solution)/shard_map/ppermute | solution.py:18
  29.2 1.5 %select_reduce_fusion = f32[8,64,256]{2,1,0:T(8,128)S(1)} fusion(f32[4]{0:T(128)} %param.11, s32[8,64,256]{2,1,0:T(8,128)} %param.10), kind=kLoop, calls=%fused_computation.22 | loop fusion | flops 1441792 | bytes 1048592 | tf_op jit(solution)/shard_map/reduce_sum | solution.py:45
  30.8 1.2 %select_reduce_fusion.1 = f32[4]{0:T(128)S(1)} fusion(f32[8]{0:T(128)} %param.13, s32[4]{0:T(128)} %param.12), kind=kLoop, calls=%fused_computation.48 | loop fusion | flops 92 | bytes 64 | tf_op jit(solution)/shard_map/reduce_sum | solution.py:50
  32.0 1.4 %select_maximum_fusion.2 = f32[10,66,258]{2,1,0:T(8,128)S(1)} fusion(f32[1,64,256]{2,1,0:T(8,128)S(1)} %collective-permute-done, f32[8,64,256]{2,1,0:T(8,128)} %param.7, f32[1,64,256]{2,1,0:T(8,128)S(1)} %collective-permute-done.1), kind=kLoop, calls=%fused_computation.30 | loop fusion | flops 2554200 | bytes 1336480 | tf_op jit(solution)/shard_map/concatenate | solution.py:19
  33.4 0.5 fusion.15
  34.0 0.1 pad_maximum_fusion.2
  34.1 1.1 multiply_reduce_fusion
  35.2 0.0 copy-done.2
  35.2 2.6 %fusion.19 = (f32[8,64,256]{2,1,0:T(8,128)}, f32[4,8,64,256]{3,2,1,0:T(8,128)}) fusion(bf16[4,8,64,256]{3,2,1,0:T(8,128)(2,1)S(1)} %copy-done.2, f32[4]{0:T(128)S(1)} %select_reduce_fusion.1, f32[4,8,64,256]{3,2,1,0:T(8,128)S(1)} %multiply_reduce_fusion, f32[8,64,256]{2,1,0:T(8,128)S(1)} %copy-done.1), kind=kLoop, calls=%fused_computation.50 | loop fusion | flops 2490368 | bytes 6291472 | tf_op jit(solution)/shard_map/reduce_sum | solution.py:57
  37.8 0.0 reduce-scatter.2.cloned.1.call-update
  37.9 1.1 collective-permute-done.2
  39.0 10.8 %select_maximum_fusion = f32[4,3,10,66,258]{4,3,2,1,0:T(8,128)} fusion(f32[4,3,1,64,256]{4,3,2,1,0:T(8,128)} %collective-permute-done.2, f32[4,3,8,64,256]{4,3,2,1,0:T(8,128)} %param.9, f32[4,3,1,64,256]{4,3,2,1,0:T(8,128)S(1)} %collective-permute-done.3), kind=kLoop, calls=%fused_computation.4 | loop fusion | flops 30650400 | bytes 16037760 | tf_op jit(solution)/shard_map/concatenate | solution.py:19
  49.8 26.3 %reduce-scatter.2.cloned.1.call-done = f32[8,8,256]{2,1,0:T(8,128)} async-done(((f32[8,64,256]{2,1,0:T(8,128)}), f32[8,8,256]{2,1,0:T(8,128)}) %reduce-scatter.2.cloned.1.call-update) | async-done | bytes 65552 | tf_op jit(solution)/shard_map/reduce_scatter | solution.py:59
  76.1 0.8 multiply_subtract_fusion.1
  76.9 0.8 stack.27
  77.8 3.5 %all-to-all-start = ((f32[8,8,8,256]{3,2,1,0:T(8,128)}), f32[8,8,8,256]{3,2,1,0:T(8,128)S(1)}, u32[]{:S(2)}, u32[]{:S(2)}) async-start(f32[8,8,8,256]{3,2,1,0:T(8,128)} %stack.27), calls=%async_computation.1 | async-start | bytes 1048576 | tf_op jit(solution)/shard_map/all_to_all | solution.py:63
  81.3 25.7 %fusion.7 = f32[4,3,8,64,256]{4,3,2,1,0:T(8,128)} fusion(f32[4,3,8,64,256]{4,3,2,1,0:T(8,128)} %param.9, f32[4,3,10,66,258]{4,3,2,1,0:T(8,128)} %select_maximum_fusion, f32[4,3,1,64,256]{4,3,2,1,0:T(8,128)S(1)} %collective-permute-done.3, f32[4,3,1,64,256]{4,3,2,1,0:T(8,128)} %collective-permute-done.2, f32[8,64,256]{2,1,0:T(8,128)S(1)} %select_reduce_fusion, ...), kind=kLoop, calls=%fused_computation.14 | loop fusion | flops 22020096 | bytes 43515904 | tf_op jit(solution)/shard_map/sub | solution.py:56
  107.0 0.8 copy.12
  (10 shorter events, 0.1 us)
Async XLA Ops:
  7.2 26.7 %copy-start.1 = (f32[8,64,256]{2,1,0:T(8,128)S(1)}, f32[8,64,256]{2,1,0:T(8,128)}, u32[]{:S(2)}) copy-start(f32[8,64,256]{2,1,0:T(8,128)} %param.7) | copy-start | bytes 1572868
  7.2 68.9 %reduce-scatter.2.cloned.1.call-start = ((), (), s32[]{:S(2)}) async-start(), calls=%async_computation.2 | async-start | bytes 589824 | tf_op jit(solution)/shard_map/reduce_scatter | solution.py:59
  8.2 23.8 %collective-permute-start.1 = (f32[1,64,256]{2,1,0:T(8,128)S(1)}, f32[1,64,256]{2,1,0:T(8,128)S(1)}, u32[]{:S(2)}, u32[]{:S(2)}) collective-permute-start(f32[1,64,256]{2,1,0:T(8,128)S(1)} %get-tuple-element.8), channel_id=1, source_target_pairs={{0,1},{1,2},{2,3},{3,4},{4,5},{5,6},{6,7},{7,8},{8,9},{9,10},{10,1... | collective-permute-start | bytes 196616 | tf_op jit(solution)/shard_map/ppermute | solution.py:15
  10.1 21.9 %collective-permute-start = (f32[1,64,256]{2,1,0:T(8,128)S(1)}, f32[1,64,256]{2,1,0:T(8,128)S(1)}, u32[]{:S(2)}, u32[]{:S(2)}) collective-permute-start(f32[1,64,256]{2,1,0:T(8,128)S(1)} %get-tuple-element.9), channel_id=1, source_target_pairs={{1,0},{2,1},{3,2},{4,3},{5,4},{6,5},{7,6},{8,7},{9,8},{10,9},{11,1... | collective-permute-start | bytes 196616 | tf_op jit(solution)/shard_map/ppermute | solution.py:18
  20.0 17.8 %collective-permute-start.3 = (f32[4,3,1,64,256]{4,3,2,1,0:T(8,128)}, f32[4,3,1,64,256]{4,3,2,1,0:T(8,128)S(1)}, u32[]{:S(2)}, u32[]{:S(2)}) collective-permute-start(f32[4,3,1,64,256]{4,3,2,1,0:T(8,128)} %get-tuple-element.4), channel_id=1, source_target_pairs={{0,1},{1,2},{2,3},{3,4},{4,5},{5,6},{6,7},{7,8},{8,9},{9,10},{10,1... | collective-permute-start | bytes 2359304 | tf_op jit(solution)/shard_map/ppermute | solution.py:15
  21.9 17.1 %collective-permute-start.2 = (f32[4,3,1,64,256]{4,3,2,1,0:T(8,128)}, f32[4,3,1,64,256]{4,3,2,1,0:T(8,128)}, u32[]{:S(2)}, u32[]{:S(2)}) collective-permute-start(f32[4,3,1,64,256]{4,3,2,1,0:T(8,128)} %get-tuple-element.5), channel_id=1, source_target_pairs={{1,0},{2,1},{3,2},{4,3},{5,4},{6,5},{7,6},{8,7},{9,8},{10,9},{11,1... | collective-permute-start | bytes 2359304 | tf_op jit(solution)/shard_map/ppermute | solution.py:18
  29.2 4.9 %copy-start = (f32[4,3,8,64,256]{4,3,2,1,0:T(8,128)S(1)}, f32[4,3,8,64,256]{4,3,2,1,0:T(8,128)}, u32[]{:S(2)}) copy-start(f32[4,3,8,64,256]{4,3,2,1,0:T(8,128)} %param.9) | copy-start | bytes 18874372
  34.0 1.2 %copy-start.2 = (bf16[4,8,64,256]{3,2,1,0:T(8,128)(2,1)S(1)}, bf16[4,8,64,256]{3,2,1,0:T(8,128)(2,1)}, u32[]{:S(2)}) copy-start(bf16[4,8,64,256]{3,2,1,0:T(8,128)(2,1)} %param.8) | copy-start | bytes 3145732
  77.8 29.2 %all-to-all-start = ((f32[8,8,8,256]{3,2,1,0:T(8,128)}), f32[8,8,8,256]{3,2,1,0:T(8,128)S(1)}, u32[]{:S(2)}, u32[]{:S(2)}) async-start(f32[8,8,8,256]{3,2,1,0:T(8,128)} %stack.27), calls=%async_computation.1 | async-start | bytes 1048576 | tf_op jit(solution)/shard_map/all_to_all | solution.py:63
Sparse Core Ops, SparseCore 0:
  38.0 38.0 reduce-scatter.1
